TPU v7x, 32 devices: a whole 2x2x4 slice. The times are simulated.
32 devices in a mesh: gx: 2 (over y), gy: 4 (over x, core), gz: 4 (over z).
Axes of the slice: x: 2, y: 2, z: 4, core: 2. Of those that a mesh axis runs over, the one named last changes fastest.
Arguments:
- tokens: bfloat16 [256, 8192], P('gx', 'gy'), may hold values from -6 to 6
- cotangent: bfloat16 [256, 8192], P('gx', 'gy'), may hold values from -6 to 6
- gate_weight: bfloat16 [8192, 28672], P('gy', ('gx', 'gz')), may hold values from -5.7452426 to 5.7452426
- up_weight: bfloat16 [8192, 28672], P('gy', ('gx', 'gz')), may hold values from -5.7452426 to 5.7452426
- down_weight: bfloat16 [28672, 8192], P(('gx', 'gz'), 'gy'), may hold values from -3.0709613 to 3.0709613
- gate_reduce: bfloat16 [8192, 32], P('gy'), may hold values from -0.0625 to 0.0625
- gate_expand: bfloat16 [32, 28672], P(None, ('gx', 'gz')), may hold values from -5 to 5
- gate_magnitude: float32 [28672], P(('gx', 'gz')), may hold values from 0.5 to 2
- up_reduce: bfloat16 [8192, 32], P('gy'), may hold values from -0.0625 to 0.0625
- up_expand: bfloat16 [32, 28672], P(None, ('gx', 'gz')), may hold values from -5 to 5
- up_magnitude: float32 [28672], P(('gx', 'gz')), may hold values from 0.5 to 2
- down_reduce: bfloat16 [28672, 32], P(('gx', 'gz')), may hold values from -0.03125 to 0.03125
- down_expand: bfloat16 [32, 8192], P(None, 'gy'), may hold values from -5 to 5
- down_magnitude: float32 [8192], P('gy'), may hold values from 0.5 to 2
Outputs:
- output: bfloat16 [256, 8192], P('gx', 'gy')
- grad_tokens: bfloat16 [256, 8192], P('gx', 'gy')
- grad_gate_reduce: float32 [8192, 32], P('gy')
- grad_gate_expand: float32 [32, 28672], P(None, ('gx', 'gz'))
- grad_gate_magnitude: float32 [28672], P(('gx', 'gz'))
- grad_up_reduce: float32 [8192, 32], P('gy')
- grad_up_expand: float32 [32, 28672], P(None, ('gx', 'gz'))
- grad_up_magnitude: float32 [28672], P(('gx', 'gz'))
- grad_down_reduce: float32 [28672, 32], P(('gx', 'gz'))
- grad_down_expand: float32 [32, 8192], P(None, 'gy')
- grad_down_magnitude: float32 [8192], P('gy')
All inputs are finite; a program needn't handle non-finite values.
Results may differ from a plain program's by a relative error of at most 0.012.
Values may be sent and summed in bfloat16 or wider, within the bound.
No kernel may reach another device: no remote copies, remote signals or barrier semaphores. Data moves between devices by JAX's collectives and lax.ppermute only.
A program may use at most 128 MiB of HBM per device.

v0:
```python
import jax
import jax.numpy as jnp
from jax import lax
from jax.sharding import PartitionSpec as P

EPSILON = 1e-06


def tile_square(weight, reduce_in, expand_out):
    merged = weight.astype(jnp.float32) + jnp.dot(
        reduce_in, expand_out, preferred_element_type=jnp.float32
    )
    return jnp.sum(merged * merged, axis=0)


def share_rows(values, count):
    return lax.dynamic_slice_in_dim(values, lax.axis_index("gz") * count, count, 0)


def contract_last(left, right):
    return lax.dot_general(
        left, right, (((1,), (1,)), ((), ())), preferred_element_type=jnp.float32
    )


def contract_first(left, right):
    return lax.dot_general(
        left, right, (((0,), (0,)), ((), ())), preferred_element_type=jnp.float32
    )


def on_device(
    tokens,
    cotangent,
    gate_weight,
    up_weight,
    down_weight,
    gate_reduce,
    gate_expand,
    gate_magnitude,
    up_reduce,
    up_expand,
    up_magnitude,
    down_reduce,
    down_expand,
    down_magnitude,
):
    share_count = tokens.shape[0] // lax.axis_size("gz")
    square_gate = tile_square(gate_weight, gate_reduce, gate_expand)
    square_up = tile_square(up_weight, up_reduce, up_expand)
    square_down = tile_square(down_weight, down_reduce, down_expand)
    norm_down = jnp.sqrt(lax.psum(square_down, ("gx", "gz")) + EPSILON)
    scale_down = down_magnitude / norm_down
    all_tokens = lax.all_gather(tokens, "gx", axis=0, tiled=True)
    part_gate = jnp.dot(all_tokens, gate_weight, preferred_element_type=jnp.float32)
    part_up = jnp.dot(all_tokens, up_weight, preferred_element_type=jnp.float32)
    low_gate_part = jnp.dot(all_tokens, gate_reduce, preferred_element_type=jnp.float32)
    low_up_part = jnp.dot(all_tokens, up_reduce, preferred_element_type=jnp.float32)
    gate_lin, up_lin, gate_lowsum, up_lowsum = (
        lax.psum_scatter(part_gate, "gy", scatter_dimension=0, tiled=True),
        lax.psum_scatter(part_up, "gy", scatter_dimension=0, tiled=True),
        lax.psum_scatter(low_gate_part, "gy", scatter_dimension=0, tiled=True),
        lax.psum_scatter(low_up_part, "gy", scatter_dimension=0, tiled=True),
    )
    summed_gate, summed_up = lax.psum((square_gate, square_up), "gy")
    norm_gate = jnp.sqrt(summed_gate + EPSILON)
    norm_up = jnp.sqrt(summed_up + EPSILON)
    scale_gate = gate_magnitude / norm_gate
    scale_up = up_magnitude / norm_up
    gate_low = gate_lowsum.astype(jnp.bfloat16)
    up_low = up_lowsum.astype(jnp.bfloat16)
    gate_lin = gate_lin + jnp.dot(gate_low, gate_expand, preferred_element_type=jnp.float32)
    up_lin = up_lin + jnp.dot(up_low, up_expand, preferred_element_type=jnp.float32)
    gate_pre = gate_lin * scale_gate[None, :]
    up_pre = up_lin * scale_up[None, :]
    sigmoid_gate = jax.nn.sigmoid(gate_pre)
    active = gate_pre * sigmoid_gate
    hidden = (active * up_pre).astype(jnp.bfloat16)
    all_hidden = lax.all_gather(hidden, "gy", axis=0, tiled=True)
    part_down = jnp.dot(all_hidden, down_weight, preferred_element_type=jnp.float32)
    low_down_part = jnp.dot(all_hidden, down_reduce, preferred_element_type=jnp.float32)
    down_lin, down_lowsum = (
        lax.psum_scatter(part_down, "gx", scatter_dimension=0, tiled=True),
        lax.psum_scatter(low_down_part, "gx", scatter_dimension=0, tiled=True),
    )
    down_lin, down_lowsum = lax.psum((down_lin, down_lowsum), "gz")
    down_low = down_lowsum.astype(jnp.bfloat16)
    down_lin = down_lin + jnp.dot(down_low, down_expand, preferred_element_type=jnp.float32)
    output = (down_lin * scale_down[None, :]).astype(jnp.bfloat16)
    down_lin = share_rows(down_lin, share_count)
    down_low = share_rows(down_low, share_count)
    cot_float = cotangent.astype(jnp.float32)
    down_delta = (cot_float * scale_down[None, :]).astype(jnp.bfloat16)
    cot_share = share_rows(cot_float, share_count)
    delta_share = share_rows(down_delta, share_count)
    grad_down_magnitude = jnp.sum(cot_share * down_lin, axis=0) / norm_down
    grad_down_expand = contract_first(down_low, delta_share)
    grad_down_magnitude, grad_down_expand = lax.psum(
        (grad_down_magnitude, grad_down_expand), ("gx", "gz")
    )
    all_delta = lax.all_gather(down_delta, "gx", axis=0, tiled=True)
    part_hidden_grad = contract_last(all_delta, down_weight)
    part_down_back = contract_last(all_delta, down_expand)
    hidden_gradsum, down_backsum = (
        lax.psum_scatter(part_hidden_grad, "gy", scatter_dimension=0, tiled=True),
        lax.psum_scatter(part_down_back, "gy", scatter_dimension=0, tiled=True),
    )
    down_back = down_backsum.astype(jnp.bfloat16)
    hidden_grad = (hidden_gradsum + contract_last(down_back, down_reduce)).astype(jnp.bfloat16)
    grad_down_reduce = contract_first(hidden, down_back)
    hgrad_float = hidden_grad.astype(jnp.float32)
    gate_grad = hgrad_float * up_pre * sigmoid_gate * (1.0 + gate_pre * (1.0 - sigmoid_gate))
    up_grad = hgrad_float * active
    gate_delta = (gate_grad * scale_gate[None, :]).astype(jnp.bfloat16)
    up_delta = (up_grad * scale_up[None, :]).astype(jnp.bfloat16)
    grad_gate_magnitude = jnp.sum(gate_grad * gate_lin, axis=0) / norm_gate
    grad_up_magnitude = jnp.sum(up_grad * up_lin, axis=0) / norm_up
    grad_gate_expand = contract_first(gate_low, gate_delta)
    grad_up_expand = contract_first(up_low, up_delta)
    grad_down_reduce, grad_gate_magnitude, grad_up_magnitude, grad_gate_expand, grad_up_expand = (
        lax.psum(
            (
                grad_down_reduce,
                grad_gate_magnitude,
                grad_up_magnitude,
                grad_gate_expand,
                grad_up_expand,
            ),
            "gy",
        )
    )
    all_gate_delta, all_up_delta = (
        lax.all_gather(gate_delta, "gy", axis=0, tiled=True),
        lax.all_gather(up_delta, "gy", axis=0, tiled=True),
    )
    part_input = contract_last(all_gate_delta, gate_weight) + contract_last(all_up_delta, up_weight)
    part_gate_back = contract_last(all_gate_delta, gate_expand)
    part_up_back = contract_last(all_up_delta, up_expand)
    input_sum, gate_backsum, up_backsum = (
        lax.psum_scatter(part_input, "gx", scatter_dimension=0, tiled=True),
        lax.psum_scatter(part_gate_back, "gx", scatter_dimension=0, tiled=True),
        lax.psum_scatter(part_up_back, "gx", scatter_dimension=0, tiled=True),
    )
    input_sum, gate_backsum, up_backsum = lax.psum((input_sum, gate_backsum, up_backsum), "gz")
    gate_back = gate_backsum.astype(jnp.bfloat16)
    up_back = up_backsum.astype(jnp.bfloat16)
    grad_tokens = (
        input_sum + contract_last(gate_back, gate_reduce) + contract_last(up_back, up_reduce)
    ).astype(jnp.bfloat16)
    gate_back = share_rows(gate_back, share_count)
    up_back = share_rows(up_back, share_count)
    token_share = share_rows(tokens, share_count)
    grad_gate_reduce = contract_first(token_share, gate_back)
    grad_up_reduce = contract_first(token_share, up_back)
    grad_gate_reduce, grad_up_reduce = lax.psum((grad_gate_reduce, grad_up_reduce), ("gx", "gz"))
    return (
        output,
        grad_tokens,
        grad_gate_reduce,
        grad_gate_expand,
        grad_gate_magnitude,
        grad_up_reduce,
        grad_up_expand,
        grad_up_magnitude,
        grad_down_reduce,
        grad_down_expand,
        grad_down_magnitude,
    )


def solution(mesh):
    return jax.shard_map(
        on_device,
        mesh=mesh,
        in_specs=(
            P("gx", "gy"),
            P("gx", "gy"),
            P("gy", ("gx", "gz")),
            P("gy", ("gx", "gz")),
            P(("gx", "gz"), "gy"),
            P("gy", None),
            P(None, ("gx", "gz")),
            P(("gx", "gz")),
            P("gy", None),
            P(None, ("gx", "gz")),
            P(("gx", "gz")),
            P(("gx", "gz"), None),
            P(None, "gy"),
            P("gy"),
        ),
        out_specs=(
            P("gx", "gy"),
            P("gx", "gy"),
            P("gy", None),
            P(None, ("gx", "gz")),
            P(("gx", "gz")),
            P("gy", None),
            P(None, ("gx", "gz")),
            P(("gx", "gz")),
            P(("gx", "gz"), None),
            P(None, "gy"),
            P("gy"),
        ),
        check_vma=False,
    )
```

profile of v0, /device:TPU:0, one launch (start us, length us, event | category | flops | bytes accessed | tf_op | source)
XLA Modules:
  0.0 689.7 jit_solution(911645773237748030)
XLA Ops:
  7.3 9.5 %multiply_reduce_fusion = f32[2048]{0:T(1024)S(1)} fusion(bf16[3584,2048]{1,0:T(8,128)(2,1)} %param.18, bf16[3584,32]{0,1:T(8,128)(2,1)} %param.25, bf16[32,2048]{1,0:T(8,128)(2,1)} %param.26), kind=kOutput, calls=%fused_computation | convolution fusion | flops 499120128 | bytes 15048704 | tf_op jit(solution)/shard_map/dot_general | solution.py:10
  16.8 23.7 %psum.123 = f32[2048]{0:T(1024)S(1)} all-reduce(f32[2048]{0:T(1024)S(1)} %multiply_reduce_fusion), channel_id=1, replica_groups=mesh['gx'=2,'gy'=4,'gz'=4] {'gx','gz'}, use_global_device_ids=true, to_apply=%region_13.0 | all-reduce | flops 2048 | bytes 16384 | tf_op jit(solution)/shard_map/psum | solution.py:52
  42.3 17.9 %all-gather.10.cloned.1.call-done = bf16[256,2048]{1,0:T(8,128)(2,1)} async-done(((bf16[128,2048]{1,0:T(8,128)(2,1)}), bf16[256,2048]{1,0:T(8,128)(2,1)}) %all-gather.10.cloned.1.call-update) | async-done | bytes 1048592 | tf_op jit(solution)/shard_map/all_gather | solution.py:101
  60.2 2.3 fusion.38
  62.6 20.5 %all-gather.6.cloned.1.call-done = bf16[256,2048]{1,0:T(8,128)(2,1)} async-done(((bf16[128,2048]{1,0:T(8,128)(2,1)}), bf16[256,2048]{1,0:T(8,128)(2,1)}) %all-gather.6.cloned.1.call-update) | async-done | bytes 1048592 | tf_op jit(solution)/shard_map/all_gather | solution.py:54
  83.0 2.3 fusion.32
  85.4 2.3 fusion.34
  87.8 11.4 %fusion.37 = f32[256,3584]{1,0:T(8,128)} fusion(bf16[256,2048]{1,0:T(8,128)(2,1)} %all-gather.10.cloned.1.call-done, bf16[3584,2048]{1,0:T(8,128)(2,1)} %param.18), kind=kOutput, calls=%fused_computation.60 | convolution fusion | flops 3758096384 | bytes 19398656 | tf_op jit(solution)/shard_map/dot_general | solution.py:21
  99.3 9.1 %fusion.31 = f32[256,3584]{1,0:T(8,128)} fusion(bf16[256,2048]{1,0:T(8,128)(2,1)S(1)} %copy-done.1, bf16[2048,3584]{1,0:T(8,128)(2,1)} %param.16), kind=kOutput, calls=%fused_computation.54 | convolution fusion | flops 3758096384 | bytes 19398656 | tf_op jit(solution)/shard_map/dot_general | solution.py:55
  108.7 9.2 %fusion.33 = f32[256,3584]{1,0:T(8,128)} fusion(bf16[256,2048]{1,0:T(8,128)(2,1)S(1)} %copy-done.1, bf16[2048,3584]{1,0:T(8,128)(2,1)} %param.17), kind=kOutput, calls=%fused_computation.56 | convolution fusion | flops 3758096384 | bytes 19398656 | tf_op jit(solution)/shard_map/dot_general | solution.py:56
  117.9 7.5 %multiply_reduce_fusion.1 = f32[3584]{0:T(1024)S(1)} fusion(bf16[2048,3584]{1,0:T(8,128)(2,1)} %param.17, bf16[2048,32]{0,1:T(8,128)(2,1)S(1)} %copy-done.10, bf16[32,3584]{1,0:T(8,128)(2,1)S(1)} %copy-done), kind=kOutput, calls=%fused_computation.1 | convolution fusion | flops 499118592 | bytes 15054848 | tf_op jit(solution)/shard_map/dot_general | solution.py:10
  125.5 7.6 %multiply_reduce_fusion.2 = f32[3584]{0:T(1024)S(1)} fusion(bf16[2048,3584]{1,0:T(8,128)(2,1)} %param.16, bf16[2048,32]{0,1:T(8,128)(2,1)S(1)} %copy-done.9, bf16[32,3584]{1,0:T(8,128)(2,1)S(1)} %copy-done.7), kind=kOutput, calls=%fused_computation.2 | convolution fusion | flops 499118592 | bytes 15054848 | tf_op jit(solution)/shard_map/dot_general | solution.py:10
  133.1 10.9 %all-reduce.4 = (f32[3584]{0:T(1024)S(1)}, f32[3584]{0:T(1024)S(1)}) all-reduce(f32[3584]{0:T(1024)S(1)} %multiply_reduce_fusion.1, f32[3584]{0:T(1024)S(1)} %multiply_reduce_fusion.2), channel_id=1, replica_groups=mesh['gx'=2,'gy'=4,'gz'=4] {'gy'}, use_global_device_ids=true, to_apply=%region_7.0 | all-reduce | flops 7168 | bytes 57344 | tf_op jit(solution)/shard_map/psum | solution.py:65
  146.3 4.5 reduce-scatter.36.cloned.1.call-done
  151.6 42.8 %reduce-scatter.26.cloned.1.call-done = f32[64,3584]{1,0:T(8,128)} async-done(((f32[256,3584]{1,0:T(8,128)}), f32[64,3584]{1,0:T(8,128)}) %reduce-scatter.26.cloned.1.call-update) | async-done | bytes 917520 | tf_op jit(solution)/shard_map/reduce_scatter | solution.py:105
  195.9 42.3 %reduce-scatter.18.cloned.1.call-done = f32[64,3584]{1,0:T(8,128)} async-done(((f32[256,3584]{1,0:T(8,128)}), f32[64,3584]{1,0:T(8,128)}) %reduce-scatter.18.cloned.1.call-update) | async-done | bytes 917520 | tf_op jit(solution)/shard_map/reduce_scatter | solution.py:60
  238.2 1.5 convolution_add_fusion.2
  239.7 42.3 %reduce-scatter.20.cloned.1.call-done = f32[64,3584]{1,0:T(8,128)} async-done(((f32[256,3584]{1,0:T(8,128)}), f32[64,3584]{1,0:T(8,128)}) %reduce-scatter.20.cloned.1.call-update) | async-done | bytes 917520 | tf_op jit(solution)/shard_map/reduce_scatter | solution.py:61
  282.1 3.5 multiply_reduce_fusion.3
  288.0 19.6 %all-gather.12.cloned.1.call-done = bf16[256,3584]{1,0:T(8,128)(2,1)} async-done(((bf16[64,3584]{1,0:T(8,128)(2,1)}), bf16[256,3584]{1,0:T(8,128)(2,1)}) %all-gather.12.cloned.1.call-update) | async-done | bytes 1835024 | tf_op jit(solution)/shard_map/all_gather | solution.py:133
  307.7 11.0 %fusion.39 = f32[256,2048]{1,0:T(8,128)} fusion(bf16[256,3584]{1,0:T(8,128)(2,1)} %all-gather.12.cloned.1.call-done, bf16[2048,3584]{1,0:T(8,128)(2,1)} %param.16), kind=kOutput, calls=%fused_computation.62 | convolution fusion | flops 3758096384 | bytes 18612224 | tf_op jit(solution)/shard_map/dot_general | solution.py:21
  318.7 12.1 %all-gather.14.cloned.1.call-done = bf16[256,3584]{1,0:T(8,128)(2,1)} async-done(((bf16[64,3584]{1,0:T(8,128)(2,1)}), bf16[256,3584]{1,0:T(8,128)(2,1)}) %all-gather.14.cloned.1.call-update) | async-done | bytes 1835024 | tf_op jit(solution)/shard_map/all_gather | solution.py:134
  330.8 11.6 %convolution_add_fusion.3 = f32[256,2048]{1,0:T(8,128)} fusion(f32[256,2048]{1,0:T(8,128)} %fusion.39, bf16[256,3584]{1,0:T(8,128)(2,1)} %all-gather.14.cloned.1.call-done, bf16[2048,3584]{1,0:T(8,128)(2,1)} %param.17), kind=kOutput, calls=%fused_computation.8 | convolution fusion | flops 3758620672 | bytes 20709376 | tf_op jit(solution)/shard_map/dot_general | solution.py:21
  342.5 11.6 %all-gather.8.cloned.1.call-done = bf16[256,3584]{1,0:T(8,128)(2,1)} async-done(((bf16[64,3584]{1,0:T(8,128)(2,1)}), bf16[256,3584]{1,0:T(8,128)(2,1)}) %all-gather.8.cloned.1.call-update) | async-done | bytes 1835024 | tf_op jit(solution)/shard_map/all_gather | solution.py:79
  354.1 11.0 %fusion.35 = f32[256,2048]{1,0:T(8,128)} fusion(bf16[256,3584]{1,0:T(8,128)(2,1)} %all-gather.8.cloned.1.call-done, bf16[3584,2048]{1,0:T(8,128)(2,1)} %param.18), kind=kOutput, calls=%fused_computation.58 | convolution fusion | flops 3758096384 | bytes 18612224 | tf_op jit(solution)/shard_map/dot_general | solution.py:80
  365.2 2.8 fusion.40
  368.0 2.7 fusion.36
  370.9 2.8 fusion.41
  373.7 14.4 %reduce-scatter.28.cloned.1.call-done = f32[128,2048]{1,0:T(8,128)} async-done(((f32[256,2048]{1,0:T(8,128)}), f32[128,2048]{1,0:T(8,128)}) %reduce-scatter.28.cloned.1.call-update) | async-done | bytes 1048592 | tf_op jit(solution)/shard_map/reduce_scatter | solution.py:140
  388.1 34.2 %reduce-scatter.22.cloned.1.call-done = f32[128,2048]{1,0:T(8,128)} async-done(((f32[256,2048]{1,0:T(8,128)}), f32[128,2048]{1,0:T(8,128)}) %reduce-scatter.22.cloned.1.call-update) | async-done | bytes 1048592 | tf_op jit(solution)/shard_map/reduce_scatter | solution.py:83
  424.3 1.7 fusion.43
  427.0 11.5 %all-reduce.3 = (f32[3584]{0:T(1024)}, f32[3584]{0:T(1024)}) all-reduce(f32[3584]{0:T(1024)S(1)} %get-tuple-element.33, f32[3584]{0:T(1024)S(1)} %get-tuple-element.34), channel_id=1, replica_groups=mesh['gx'=2,'gy'=4,'gz'=4] {'gy'}, use_global_device_ids=true, to_apply=%region_25.0 | all-reduce | flops 7168 | bytes 57344 | tf_op jit(solution)/shard_map/psum | solution.py:121
  438.5 9.1 %reduce-scatter.24.cloned.1.call-done = f32[128,32]{0,1:T(8,128)} async-done(((f32[256,32]{0,1:T(8,128)}), f32[128,32]{0,1:T(8,128)}) %reduce-scatter.24.cloned.1.call-update) | async-done | bytes 16400 | tf_op jit(solution)/shard_map/reduce_scatter | solution.py:84
  447.5 12.6 %reduce-scatter.32.cloned.1.call-done = f32[128,32]{0,1:T(8,128)} async-done(((f32[256,32]{0,1:T(8,128)}), f32[128,32]{0,1:T(8,128)}) %reduce-scatter.32.cloned.1.call-update) | async-done | bytes 16400 | tf_op jit(solution)/shard_map/reduce_scatter | solution.py:142
  460.1 21.1 %all-reduce.1 = (bf16[128,32]{0,1:T(8,128)(2,1)S(1)}, bf16[128,32]{0,1:T(8,128)(2,1)S(1)}, bf16[128,32]{0,1:T(8,128)(2,1)S(1)}) all-reduce(f32[128,32]{0,1:T(8,128)} %reduce-scatter.24.cloned.1.call-done, f32[128,32]{0,1:T(8,128)} %reduce-scatter.30.cloned.1.call-done, ...), channel_id=1, replica_groups=mesh['gx'=2,'gy'=4,'gz'=4] {'gz'}, use_global_device_ids=true, to_apply=%region_11.0 | all-reduce | flops 12288 | bytes 73728 | tf_op jit(solution)/shard_map/psum | solution.py:86
  481.3 1.8 fusion.4
  485.0 64.4 %all-reduce.12.cloned.1.call-done = (f32[128,2048]{1,0:T(8,128)}, f32[128,2048]{1,0:T(8,128)}) async-done(((f32[128,2048]{1,0:T(8,128)}, f32[128,2048]{1,0:T(8,128)}), (f32[128,2048]{1,0:T(8,128)}, f32[128,2048]{1,0:T(8,128)})) %all-reduce.12.cloned.1.call-update) | async-done | bytes 2097168 | tf_op jit(solution)/shard_map/psum | solution.py:86
  549.4 2.3 multiply_convert_fusion.1
  551.8 20.5 %psum.135 = f32[2048]{0:T(1024)} all-reduce(f32[2048]{0:T(1024)S(1)} %fusion.17), channel_id=1, replica_groups=mesh['gx'=2,'gy'=4,'gz'=4] {'gx','gz'}, use_global_device_ids=true, to_apply=%region_33.0 | all-reduce | flops 2048 | bytes 16384 | tf_op jit(solution)/shard_map/psum | solution.py:98
  572.3 1.5 convolution_add_fusion.5
  574.9 17.2 %all-reduce.14.cloned.1.call-done = (f32[32,3584]{1,0:T(8,128)}, f32[32,3584]{1,0:T(8,128)}, f32[3584,32]{0,1:T(8,128)}) async-done(((f32[32,3584]{1,0:T(8,128)}, f32[32,3584]{1,0:T(8,128)}, f32[3584,32]{0,1:T(8,128)}), (f32[32,3584]{1,0:T(8,128)}, f32[32,3584]{1,0:T(8,128)}, f32[3584,32]{0,1:T(8,128)})) %all-reduce.14.cloned.1.call-update) | async-done | bytes 1376272 | tf_op jit(solution)/shard_map/psum | solution.py:121
  592.1 80.6 %all-reduce.10.cloned.1.call-done = (f32[2048,32]{0,1:T(8,128)}, f32[2048,32]{0,1:T(8,128)}, f32[32,2048]{1,0:T(8,128)}) async-done(((f32[2048,32]{0,1:T(8,128)}, f32[2048,32]{0,1:T(8,128)}, f32[32,2048]{1,0:T(8,128)}), (f32[2048,32]{0,1:T(8,128)}, f32[2048,32]{0,1:T(8,128)}, f32[32,2048]{1,0:T(8,128)})) %all-reduce.10.cloned.1.call-update) | async-done | bytes 786448 | tf_op jit(solution)/shard_map/psum | solution.py:155
  672.7 1.7 copy.39
  674.4 1.8 copy.40
  676.2 1.7 copy.41
  677.9 1.8 copy.42
  679.7 1.8 copy.43
  681.5 1.7 copy.44
  (93 shorter events, 15.5 us)
Async XLA Ops:
  7.2 110.7 %copy-start = (bf16[32,3584]{1,0:T(8,128)(2,1)S(1)}, bf16[32,3584]{1,0:T(8,128)(2,1)}, u32[]{:S(2)}) copy-start(bf16[32,3584]{1,0:T(8,128)(2,1)} %param.23) | copy-start | bytes 688132
  7.2 33.3 %copy-start.16 = (f32[2048]{0:T(1024)S(1)}, f32[2048]{0:T(1024)}, u32[]{:S(2)}) copy-start(f32[2048]{0:T(1024)} %param.27) | copy-start | bytes 24580
  7.2 33.4 %copy-start.3 = (bf16[128,2048]{1,0:T(8,128)(2,1)S(1)}, bf16[128,2048]{1,0:T(8,128)(2,1)}, u32[]{:S(2)}) copy-start(bf16[128,2048]{1,0:T(8,128)(2,1)} %param.15) | copy-start | bytes 1572868
  7.2 53.0 %copy-start.11 = (bf16[32,2048]{1,0:T(8,128)(2,1)S(1)}, bf16[32,2048]{1,0:T(8,128)(2,1)}, u32[]{:S(2)}) copy-start(bf16[32,2048]{1,0:T(8,128)(2,1)} %param.26) | copy-start | bytes 393220
  7.2 75.8 %copy-start.9 = (bf16[2048,32]{0,1:T(8,128)(2,1)S(1)}, bf16[2048,32]{0,1:T(8,128)(2,1)}, u32[]{:S(2)}) copy-start(bf16[2048,32]{0,1:T(8,128)(2,1)} %param.19) | copy-start | bytes 393220
  7.2 78.2 %copy-start.10 = (bf16[2048,32]{0,1:T(8,128)(2,1)S(1)}, bf16[2048,32]{0,1:T(8,128)(2,1)}, u32[]{:S(2)}) copy-start(bf16[2048,32]{0,1:T(8,128)(2,1)} %param.22) | copy-start | bytes 393220
  7.2 52.9 %all-gather.10.cloned.1.call-start = ((), (), s32[]{:S(2)}) async-start(), calls=%async_computation.17 | async-start | bytes 1572864 | tf_op jit(solution)/shard_map/all_gather | solution.py:101
  41.5 41.5 %all-gather.6.cloned.1.call-start = ((), (), s32[]{:S(2)}) async-start(), calls=%async_computation.11 | async-start | bytes 1572864 | tf_op jit(solution)/shard_map/all_gather | solution.py:54
  42.2 102.3 %reduce-scatter.38.cloned.1.call-start = ((), (), s32[]{:S(2)}) async-start(), calls=%async_computation.26 | async-start | bytes 163840
  62.5 82.9 %reduce-scatter.34.cloned.1.call-start = ((), (), s32[]{:S(2)}) async-start(), calls=%async_computation.24 | async-start | bytes 163840
  85.4 65.4 %reduce-scatter.36.cloned.1.call-start = ((), (), s32[]{:S(2)}) async-start(), calls=%async_computation.25 | async-start | bytes 163840
  87.7 11.5 %copy-start.1 = (bf16[256,2048]{1,0:T(8,128)(2,1)S(1)}, bf16[256,2048]{1,0:T(8,128)(2,1)}, u32[]{:S(2)}) copy-start(bf16[256,2048]{1,0:T(8,128)(2,1)} %all-gather.6.cloned.1.call-done) | copy-start | bytes 3145732
  87.8 106.7 %reduce-scatter.26.cloned.1.call-start = ((), (), s32[]{:S(2)}) async-start(), calls=%async_computation.18 | async-start | bytes 4587520 | tf_op jit(solution)/shard_map/reduce_scatter | solution.py:105
  99.2 139.0 %reduce-scatter.18.cloned.1.call-start = ((), (), s32[]{:S(2)}) async-start(), calls=%async_computation.12 | async-start | bytes 4587520 | tf_op jit(solution)/shard_map/reduce_scatter | solution.py:60
  108.4 173.6 %reduce-scatter.20.cloned.1.call-start = ((), (), s32[]{:S(2)}) async-start(), calls=%async_computation.13 | async-start | bytes 4587520 | tf_op jit(solution)/shard_map/reduce_scatter | solution.py:61
  117.8 7.6 %copy-start.7 = (bf16[32,3584]{1,0:T(8,128)(2,1)S(1)}, bf16[32,3584]{1,0:T(8,128)(2,1)}, u32[]{:S(2)}) copy-start(bf16[32,3584]{1,0:T(8,128)(2,1)} %param.20) | copy-start | bytes 688132
  117.9 189.8 %all-gather.12.cloned.1.call-start = ((), (), s32[]{:S(2)}) async-start(), calls=%async_computation.19 | async-start | bytes 2293760 | tf_op jit(solution)/shard_map/all_gather | solution.py:133
  125.5 18.5 %copy-start.14 = (f32[3584]{0:T(1024)S(1)}, f32[3584]{0:T(1024)}, u32[]{:S(2)}) copy-start(f32[3584]{0:T(1024)} %param.21) | copy-start | bytes 43012
  125.5 18.6 %copy-start.15 = (f32[3584]{0:T(1024)S(1)}, f32[3584]{0:T(1024)}, u32[]{:S(2)}) copy-start(f32[3584]{0:T(1024)} %param.24) | copy-start | bytes 43012
  125.5 68.9 %copy-start.8 = (bf16[3584,32]{0,1:T(8,128)(2,1)S(1)}, bf16[3584,32]{0,1:T(8,128)(2,1)}, u32[]{:S(2)}) copy-start(bf16[3584,32]{0,1:T(8,128)(2,1)} %param.25) | copy-start | bytes 688132
  144.0 0.6 copy-start.12
  151.6 167.1 %copy-start.13 = (bf16[64,32]{0,1:T(8,128)(2,1)}, bf16[64,32]{0,1:T(8,128)(2,1)S(1)}, u32[]{:S(2)}) copy-start(bf16[64,32]{0,1:T(8,128)(2,1)S(1)} %copy.28) | copy-start | bytes 12292
  286.5 44.4 %all-gather.14.cloned.1.call-start = ((), (), s32[]{:S(2)}) async-start(), calls=%async_computation.20 | async-start | bytes 2293760 | tf_op jit(solution)/shard_map/all_gather | solution.py:134
  287.0 67.0 %all-gather.8.cloned.1.call-start = ((), (), s32[]{:S(2)}) async-start(), calls=%async_computation.14 | async-start | bytes 2293760 | tf_op jit(solution)/shard_map/all_gather | solution.py:79
  287.8 100.3 %reduce-scatter.28.cloned.1.call-start = ((), (), s32[]{:S(2)}) async-start(), calls=%async_computation.21 | async-start | bytes 3145728 | tf_op jit(solution)/shard_map/reduce_scatter | solution.py:140
  342.4 80.0 %copy-start.2 = (bf16[64,3584]{1,0:T(8,128)(2,1)S(1)}, bf16[64,3584]{1,0:T(8,128)(2,1)}, u32[]{:S(2)}) copy-start(bf16[64,3584]{1,0:T(8,128)(2,1)} %multiply_convert_fusion.3) | copy-start | bytes 1376260
  342.4 80.9 %copy-start.5 = (bf16[64,3584]{1,0:T(8,128)(2,1)S(1)}, bf16[64,3584]{1,0:T(8,128)(2,1)}, u32[]{:S(2)}) copy-start(bf16[64,3584]{1,0:T(8,128)(2,1)} %get-tuple-element.30) | copy-start | bytes 1376260
  342.4 81.9 %copy-start.4 = (bf16[64,3584]{1,0:T(8,128)(2,1)S(1)}, bf16[64,3584]{1,0:T(8,128)(2,1)}, u32[]{:S(2)}) copy-start(bf16[64,3584]{1,0:T(8,128)(2,1)} %get-tuple-element.29) | copy-start | bytes 1376260
  342.5 79.8 %reduce-scatter.22.cloned.1.call-start = ((), (), s32[]{:S(2)}) async-start(), calls=%async_computation.15 | async-start | bytes 3145728 | tf_op jit(solution)/shard_map/reduce_scatter | solution.py:83
  365.1 118.0 %copy-start.6 = (bf16[128,2048]{1,0:T(8,128)(2,1)S(1)}, bf16[128,2048]{1,0:T(8,128)(2,1)}, u32[]{:S(2)}) copy-start(bf16[128,2048]{1,0:T(8,128)(2,1)} %param.14) | copy-start | bytes 1572868
  365.1 73.3 %reduce-scatter.30.cloned.1.call-start = ((), (), s32[]{:S(2)}) async-start(), calls=%async_computation.22 | async-start | bytes 49152 | tf_op jit(solution)/shard_map/reduce_scatter | solution.py:141
  368.0 79.5 %reduce-scatter.24.cloned.1.call-start = ((), (), s32[]{:S(2)}) async-start(), calls=%async_computation.16 | async-start | bytes 49152 | tf_op jit(solution)/shard_map/reduce_scatter | solution.py:84
  370.8 89.3 %reduce-scatter.32.cloned.1.call-start = ((), (), s32[]{:S(2)}) async-start(), calls=%async_computation.23 | async-start | bytes 49152 | tf_op jit(solution)/shard_map/reduce_scatter | solution.py:142
  373.7 175.7 %all-reduce.12.cloned.1.call-start = ((), (), s32[]{:S(2)}) async-start(), calls=%async_computation.28 | async-start | bytes 4194304 | tf_op jit(solution)/shard_map/psum | solution.py:86
  422.3 169.8 %all-reduce.14.cloned.1.call-start = ((), (), s32[]{:S(2)}) async-start(), calls=%async_computation.29 | async-start | bytes 2752512 | tf_op jit(solution)/shard_map/psum | solution.py:121
  426.0 246.7 %all-reduce.10.cloned.1.call-start = ((), (), s32[]{:S(2)}) async-start(), calls=%async_computation.27 | async-start | bytes 1572864 | tf_op jit(solution)/shard_map/psum | solution.py:155
Sparse Core Ops, SparseCore 0:
  41.6 18.5 all-gather.9
  61.7 21.2 all-gather.5
  86.0 19.6 reduce-scatter.37
  108.5 19.6 reduce-scatter.33
  131.1 19.6 reduce-scatter.35
  153.1 41.2 reduce-scatter.25
  197.0 41.2 reduce-scatter.17
  240.8 41.2 reduce-scatter.19
  286.6 21.0 all-gather.11
  309.7 21.0 all-gather.13
  332.9 21.0 all-gather.7
  356.2 31.8 reduce-scatter.27
  390.4 31.8 reduce-scatter.21
  424.9 9.9 reduce-scatter.29
  437.5 9.9 reduce-scatter.23
  450.1 9.9 reduce-scatter.31
  462.4 86.9 all-reduce.11
  552.9 39.1 all-reduce.13
  597.0 75.6 all-reduce.9
where the time goes:
time: 691 us; the launch traced here: 690 us
  waiting for transfers between devices  448 us (65%)
  matrix products  122 us (18%)
  blocking collectives  87.7 us (13%)
  between operations  14.4 us (2%)
  local copies, waits for them, and re-layouts  13.6 us (2%)
    psum x1, waiting for transfers between devices, on_device(): lax.psum((grad_gate_reduce, grad_up_reduce), ('gx', 'gz'))  80.6 us
    psum x1, waiting for transfers between devices, on_device(): down_lin, down_lowsum = lax.psum((down_lin, down_lowsum), 'gz')  64.4 us
    dot_general x8, matrix products, contract_last(): lax.dot_general(left, right, (((1,), (1,)), ((), ())), preferred_element_...  43.7 us
    reduce_scatter x1, waiting for transfers between devices, on_device(): lax.psum_scatter(part_hidden_grad, 'gy', scatter_dimension=0, tiled=True)  42.8 us
    reduce_scatter x1, waiting for transfers between devices, on_device(): lax.psum_scatter(part_gate, 'gy', scatter_dimension=0, tiled=True)  42.3 us
    reduce_scatter x1, waiting for transfers between devices, on_device(): lax.psum_scatter(part_up, 'gy', scatter_dimension=0, tiled=True)  42.3 us
    reduce_scatter x1, waiting for transfers between devices, on_device(): lax.psum_scatter(part_down, 'gx', scatter_dimension=0, tiled=True)  34.2 us
    dot_general x3, matrix products, tile_square(): jnp.dot(reduce_in, expand_out, preferred_element_type=jnp.float32)  24.6 us
  transfers between devices with their start and end apart: 19, of which 16 were waited for; matrix products, arithmetic and copies ran while one was open for 16% of the time, Pallas kernels for 0%

commit v1 on v0

--- a/solution.py
+++ b/solution.py
@@ -4,6 +4,12 @@
 from jax.sharding import PartitionSpec as P
 
 EPSILON = 1e-06
+
+
+def open_the_fields(inputs):
+    for m in ("gx", "gz"):
+        inputs = lax.psum(inputs, axis_name=m)
+    return inputs
 
 
 def tile_square(weight, reduce_in, expand_out):
@@ -152,7 +158,7 @@
     token_share = share_rows(tokens, share_count)
     grad_gate_reduce = contract_first(token_share, gate_back)
     grad_up_reduce = contract_first(token_share, up_back)
-    grad_gate_reduce, grad_up_reduce = lax.psum((grad_gate_reduce, grad_up_reduce), ("gx", "gz"))
+    grad_gate_reduce, grad_up_reduce = open_the_fields((grad_gate_reduce, grad_up_reduce))
     return (
         output,
         grad_tokens,

time: 691 us -> 728 us (1.054)
  waiting for transfers between devices: 448 us -> 489 us
    psum x1, waiting for transfers between devices: 64.4 us -> 89.7 us  [on_device(): down_lin, down_lowsum = lax.psum((down_lin, down_lowsum), 'gz')]
    all_gather x1, waiting for transfers between devices: 20.5 us -> 0.02 us  [on_device(): all_tokens = lax.all_gather(tokens, 'gx', axis=0, tiled=True)]
    reduce_scatter x1, waiting for transfers between devices: 14.4 us -> 34 us  [on_device(): lax.psum_scatter(part_input, 'gx', scatter_dimension=0, tiled=True)]
    reduce_scatter x1, waiting for transfers between devices: 0.01 us -> 12.6 us  [on_device(): lax.psum_scatter(part_gate_back, 'gx', scatter_dimension=0, tiled=True)]
    all_gather x1, waiting for transfers between devices: 12.1 us -> 20.3 us  [on_device(): lax.all_gather(up_delta, 'gy', axis=0, tiled=True)]
    all_gather x1, waiting for transfers between devices: 11.6 us -> 19.7 us  [on_device(): all_hidden = lax.all_gather(hidden, 'gy', axis=0, tiled=True)]
    psum x1 -> x2, waiting for transfers between devices: 80.6 us -> 74.8 us  [the longest x1 74.8 us: on_device(): lax.psum((grad_down_magnitude, grad_down_expand), ('gx', 'gz'))]
  transfers between devices with their start and end apart: 19 -> 20, of which waited for: 16 -> 16; matrix products, arithmetic and copies ran while one was open for 16% -> 16% of each run, Pallas kernels for 0% -> 0%
where the time goes in v1:
time: 728 us; the launch traced here: 727 us
  waiting for transfers between devices  489 us (67%)
  matrix products  119 us (16%)
  blocking collectives  87 us (12%)
  between operations  14.8 us (2%)
  local copies, waits for them, and re-layouts  13.7 us (2%)
    psum x1, waiting for transfers between devices, on_device(): down_lin, down_lowsum = lax.psum((down_lin, down_lowsum), 'gz')  89.7 us
    psum x1, waiting for transfers between devices, on_device(): lax.psum((grad_down_magnitude, grad_down_expand), ('gx', 'gz'))  74.8 us
    reduce_scatter x1, waiting for transfers between devices, on_device(): lax.psum_scatter(part_hidden_grad, 'gy', scatter_dimension=0, tiled=True)  42.8 us
    reduce_scatter x1, waiting for transfers between devices, on_device(): lax.psum_scatter(part_gate, 'gy', scatter_dimension=0, tiled=True)  42.3 us
    reduce_scatter x1, waiting for transfers between devices, on_device(): lax.psum_scatter(part_up, 'gy', scatter_dimension=0, tiled=True)  41.4 us
    dot_general x8, matrix products, contract_last(): lax.dot_general(left, right, (((1,), (1,)), ((), ())), preferred_element_...  39.5 us
    reduce_scatter x1, waiting for transfers between devices, on_device(): lax.psum_scatter(part_input, 'gx', scatter_dimension=0, tiled=True)  34 us
    reduce_scatter x1, waiting for transfers between devices, on_device(): lax.psum_scatter(part_down, 'gx', scatter_dimension=0, tiled=True)  29.7 us
  transfers between devices with their start and end apart: 20, of which 16 were waited for; matrix products, arithmetic and copies ran while one was open for 16% of the time, Pallas kernels for 0%

profile of v1, /device:TPU:0, one launch (start us, length us, event | category | flops | bytes accessed | tf_op | source)
XLA Modules:
  0.0 727.0 jit_solution(5774637096116925505)
XLA Ops:
  8.0 9.5 %multiply_reduce_fusion = f32[2048]{0:T(1024)S(1)} fusion(bf16[3584,2048]{1,0:T(8,128)(2,1)} %param.18, bf16[3584,32]{0,1:T(8,128)(2,1)} %param.25, bf16[32,2048]{1,0:T(8,128)(2,1)} %param.26), kind=kOutput, calls=%fused_computation | convolution fusion | flops 499120128 | bytes 15048704 | tf_op jit(solution)/shard_map/dot_general | solution.py:16
  17.5 23.8 %psum.137 = f32[2048]{0:T(1024)S(1)} all-reduce(f32[2048]{0:T(1024)S(1)} %multiply_reduce_fusion), channel_id=1, replica_groups=mesh['gx'=2,'gy'=4,'gz'=4] {'gx','gz'}, use_global_device_ids=true, to_apply=%region_13.0 | all-reduce | flops 2048 | bytes 16384 | tf_op jit(solution)/shard_map/psum | solution.py:58
  42.3 2.3 fusion.34
  44.7 2.4 fusion.32
  47.2 13.8 %all-gather.10.cloned.1.call-done = bf16[256,2048]{1,0:T(8,128)(2,1)} async-done(((bf16[128,2048]{1,0:T(8,128)(2,1)}), bf16[256,2048]{1,0:T(8,128)(2,1)}) %all-gather.10.cloned.1.call-update) | async-done | bytes 1048592 | tf_op jit(solution)/shard_map/all_gather | solution.py:107
  61.0 2.3 fusion.38
  63.3 11.4 %fusion.37 = f32[256,3584]{1,0:T(8,128)} fusion(bf16[256,2048]{1,0:T(8,128)(2,1)} %all-gather.10.cloned.1.call-done, bf16[3584,2048]{1,0:T(8,128)(2,1)} %param.18), kind=kOutput, calls=%fused_computation.60 | convolution fusion | flops 3758096384 | bytes 19398656 | tf_op jit(solution)/shard_map/dot_general | solution.py:27
  74.8 9.2 %fusion.31 = f32[256,3584]{1,0:T(8,128)} fusion(bf16[256,2048]{1,0:T(8,128)(2,1)S(1)} %copy-done.1, bf16[2048,3584]{1,0:T(8,128)(2,1)} %param.16), kind=kOutput, calls=%fused_computation.54 | convolution fusion | flops 3758096384 | bytes 19398656 | tf_op jit(solution)/shard_map/dot_general | solution.py:61
  84.2 9.1 %fusion.33 = f32[256,3584]{1,0:T(8,128)} fusion(bf16[256,2048]{1,0:T(8,128)(2,1)S(1)} %copy-done.1, bf16[2048,3584]{1,0:T(8,128)(2,1)} %param.17), kind=kOutput, calls=%fused_computation.56 | convolution fusion | flops 3758096384 | bytes 19398656 | tf_op jit(solution)/shard_map/dot_general | solution.py:62
  93.4 7.6 %multiply_reduce_fusion.2 = f32[3584]{0:T(1024)S(1)} fusion(bf16[2048,3584]{1,0:T(8,128)(2,1)} %param.16, bf16[2048,32]{0,1:T(8,128)(2,1)S(1)} %copy-done.10, bf16[32,3584]{1,0:T(8,128)(2,1)S(1)} %copy-done.9), kind=kOutput, calls=%fused_computation.2 | convolution fusion | flops 499118592 | bytes 15054848 | tf_op jit(solution)/shard_map/dot_general | solution.py:16
  101.0 7.6 %multiply_reduce_fusion.1 = f32[3584]{0:T(1024)S(1)} fusion(bf16[2048,3584]{1,0:T(8,128)(2,1)} %param.17, bf16[2048,32]{0,1:T(8,128)(2,1)S(1)} %copy-done.11, bf16[32,3584]{1,0:T(8,128)(2,1)S(1)} %copy-done), kind=kOutput, calls=%fused_computation.1 | convolution fusion | flops 499118592 | bytes 15054848 | tf_op jit(solution)/shard_map/dot_general | solution.py:16
  108.6 11.0 %all-reduce.3 = (f32[3584]{0:T(1024)S(1)}, f32[3584]{0:T(1024)S(1)}) all-reduce(f32[3584]{0:T(1024)S(1)} %multiply_reduce_fusion.1, f32[3584]{0:T(1024)S(1)} %multiply_reduce_fusion.2), channel_id=1, replica_groups=mesh['gx'=2,'gy'=4,'gz'=4] {'gy'}, use_global_device_ids=true, to_apply=%region_7.0 | all-reduce | flops 7168 | bytes 57344 | tf_op jit(solution)/shard_map/psum | solution.py:71
  122.5 6.1 reduce-scatter.38.cloned.1.call-done
  129.5 42.8 %reduce-scatter.26.cloned.1.call-done = f32[64,3584]{1,0:T(8,128)} async-done(((f32[256,3584]{1,0:T(8,128)}), f32[64,3584]{1,0:T(8,128)}) %reduce-scatter.26.cloned.1.call-update) | async-done | bytes 917520 | tf_op jit(solution)/shard_map/reduce_scatter | solution.py:111
  172.3 1.5 fusion.1
  173.8 42.3 %reduce-scatter.18.cloned.1.call-done = f32[64,3584]{1,0:T(8,128)} async-done(((f32[256,3584]{1,0:T(8,128)}), f32[64,3584]{1,0:T(8,128)}) %reduce-scatter.18.cloned.1.call-update) | async-done | bytes 917520 | tf_op jit(solution)/shard_map/reduce_scatter | solution.py:66
  216.2 2.4 convolution_add_fusion.2
  218.6 41.4 %reduce-scatter.20.cloned.1.call-done = f32[64,3584]{1,0:T(8,128)} async-done(((f32[256,3584]{1,0:T(8,128)}), f32[64,3584]{1,0:T(8,128)}) %reduce-scatter.20.cloned.1.call-update) | async-done | bytes 917520 | tf_op jit(solution)/shard_map/reduce_scatter | solution.py:67
  260.0 3.9 multiply_reduce_fusion.3
  265.4 19.7 %all-gather.8.cloned.1.call-done = bf16[256,3584]{1,0:T(8,128)(2,1)} async-done(((bf16[64,3584]{1,0:T(8,128)(2,1)}), bf16[256,3584]{1,0:T(8,128)(2,1)}) %all-gather.8.cloned.1.call-update) | async-done | bytes 1835024 | tf_op jit(solution)/shard_map/all_gather | solution.py:85
  285.1 2.7 fusion.36
  287.9 20.3 %all-gather.14.cloned.1.call-done = bf16[256,3584]{1,0:T(8,128)(2,1)} async-done(((bf16[64,3584]{1,0:T(8,128)(2,1)}), bf16[256,3584]{1,0:T(8,128)(2,1)}) %all-gather.14.cloned.1.call-update) | async-done | bytes 1835024 | tf_op jit(solution)/shard_map/all_gather | solution.py:140
  308.2 2.7 fusion.41
  311.0 20.5 %all-gather.12.cloned.1.call-done = bf16[256,3584]{1,0:T(8,128)(2,1)} async-done(((bf16[64,3584]{1,0:T(8,128)(2,1)}), bf16[256,3584]{1,0:T(8,128)(2,1)}) %all-gather.12.cloned.1.call-update) | async-done | bytes 1835024 | tf_op jit(solution)/shard_map/all_gather | solution.py:139
  331.5 2.7 fusion.40
  334.3 9.8 %reduce-scatter.24.cloned.1.call-done = f32[128,32]{0,1:T(8,128)} async-done(((f32[256,32]{0,1:T(8,128)}), f32[128,32]{0,1:T(8,128)}) %reduce-scatter.24.cloned.1.call-update) | async-done | bytes 16400 | tf_op jit(solution)/shard_map/reduce_scatter | solution.py:90
  344.1 12.8 %reduce-scatter.32.cloned.1.call-done = f32[128,32]{0,1:T(8,128)} async-done(((f32[256,32]{0,1:T(8,128)}), f32[128,32]{0,1:T(8,128)}) %reduce-scatter.32.cloned.1.call-update) | async-done | bytes 16400 | tf_op jit(solution)/shard_map/reduce_scatter | solution.py:148
  356.9 12.6 %reduce-scatter.30.cloned.1.call-done = f32[128,32]{0,1:T(8,128)} async-done(((f32[256,32]{0,1:T(8,128)}), f32[128,32]{0,1:T(8,128)}) %reduce-scatter.30.cloned.1.call-update) | async-done | bytes 16400 | tf_op jit(solution)/shard_map/reduce_scatter | solution.py:147
  369.5 19.9 %all-reduce = (bf16[128,32]{0,1:T(8,128)(2,1)S(1)}, bf16[128,32]{0,1:T(8,128)(2,1)S(1)}, bf16[128,32]{0,1:T(8,128)(2,1)S(1)}) all-reduce(f32[128,32]{0,1:T(8,128)} %reduce-scatter.24.cloned.1.call-done, f32[128,32]{0,1:T(8,128)} %reduce-scatter.30.cloned.1.call-done, ...), channel_id=1, replica_groups=mesh['gx'=2,'gy'=4,'gz'=4] {'gz'}, use_global_device_ids=true, to_apply=%region_11.0 | all-reduce | flops 12288 | bytes 73728 | tf_op jit(solution)/shard_map/psum | solution.py:92
  391.6 11.3 %fusion.35 = f32[256,2048]{1,0:T(8,128)} fusion(bf16[256,3584]{1,0:T(8,128)(2,1)} %all-gather.8.cloned.1.call-done, bf16[3584,2048]{1,0:T(8,128)(2,1)} %param.18), kind=kOutput, calls=%fused_computation.58 | convolution fusion | flops 3758096384 | bytes 18612224 | tf_op jit(solution)/shard_map/dot_general | solution.py:86
  403.0 7.3 %fusion.39 = f32[256,2048]{1,0:T(8,128)S(1)} fusion(bf16[256,3584]{1,0:T(8,128)(2,1)S(1)} %copy-done.6, bf16[2048,3584]{1,0:T(8,128)(2,1)} %param.16), kind=kOutput, calls=%fused_computation.62 | convolution fusion | flops 3758096384 | bytes 18612224 | tf_op jit(solution)/shard_map/dot_general | solution.py:27
  410.4 11.2 %convolution_add_fusion.3 = f32[256,2048]{1,0:T(8,128)} fusion(f32[256,2048]{1,0:T(8,128)S(1)} %fusion.39, bf16[256,3584]{1,0:T(8,128)(2,1)} %all-gather.14.cloned.1.call-done, bf16[2048,3584]{1,0:T(8,128)(2,1)} %param.17), kind=kOutput, calls=%fused_computation.8 | convolution fusion | flops 3758620672 | bytes 20709376 | tf_op jit(solution)/shard_map/dot_general | solution.py:27
  421.7 29.7 %reduce-scatter.22.cloned.1.call-done = f32[128,2048]{1,0:T(8,128)} async-done(((f32[256,2048]{1,0:T(8,128)}), f32[128,2048]{1,0:T(8,128)}) %reduce-scatter.22.cloned.1.call-update) | async-done | bytes 1048592 | tf_op jit(solution)/shard_map/reduce_scatter | solution.py:89
  451.4 34.0 %reduce-scatter.28.cloned.1.call-done = f32[128,2048]{1,0:T(8,128)} async-done(((f32[256,2048]{1,0:T(8,128)}), f32[128,2048]{1,0:T(8,128)}) %reduce-scatter.28.cloned.1.call-update) | async-done | bytes 1048592 | tf_op jit(solution)/shard_map/reduce_scatter | solution.py:146
  488.6 11.9 %all-reduce.2 = (f32[3584]{0:T(1024)}, f32[3584]{0:T(1024)}) all-reduce(f32[3584]{0:T(1024)S(1)} %get-tuple-element.34, f32[3584]{0:T(1024)S(1)} %get-tuple-element.35), channel_id=1, replica_groups=mesh['gx'=2,'gy'=4,'gz'=4] {'gy'}, use_global_device_ids=true, to_apply=%region_26.0 | all-reduce | flops 7168 | bytes 57344 | tf_op jit(solution)/shard_map/psum | solution.py:127
  500.5 1.8 fusion.4
  502.4 89.7 %all-reduce.13.cloned.1.call-done = (f32[128,2048]{1,0:T(8,128)}, f32[128,2048]{1,0:T(8,128)}, f32[2048,32]{0,1:T(8,128)}, f32[2048,32]{0,1:T(8,128)}) async-done(((f32[128,2048]{1,0:T(8,128)}, f32[128,2048]{1,0:T(8,128)}, f32[2048,32]{0,1:T(8,128)}, f32[2048,32]{0,1:T(8,128)}), (f32[128,2048]{1,0:T(8,128)}, f32[128,2048]{1,0:T(8,128)}, f32[2048,32]{0,1:T(8,128)}, ...) | async-done | bytes 2621456 | tf_op jit(solution)/shard_map/psum | solution.py:92
  592.1 2.3 multiply_convert_fusion.1
  594.5 20.4 %psum.151 = f32[2048]{0:T(1024)} all-reduce(f32[2048]{0:T(1024)S(1)} %fusion.17), channel_id=1, replica_groups=mesh['gx'=2,'gy'=4,'gz'=4] {'gx','gz'}, use_global_device_ids=true, to_apply=%region_35.0 | all-reduce | flops 2048 | bytes 16384 | tf_op jit(solution)/shard_map/psum | solution.py:104
  614.8 1.6 convolution_add_fusion.5
  617.5 17.4 %all-reduce.15.cloned.1.call-done = (f32[32,3584]{1,0:T(8,128)}, f32[32,3584]{1,0:T(8,128)}, f32[3584,32]{0,1:T(8,128)}) async-done(((f32[32,3584]{1,0:T(8,128)}, f32[32,3584]{1,0:T(8,128)}, f32[3584,32]{0,1:T(8,128)}), (f32[32,3584]{1,0:T(8,128)}, f32[32,3584]{1,0:T(8,128)}, f32[3584,32]{0,1:T(8,128)})) %all-reduce.15.cloned.1.call-update) | async-done | bytes 1376272 | tf_op jit(solution)/shard_map/psum | solution.py:127
  634.9 74.8 %all-reduce.11.cloned.1.call-done = f32[32,2048]{1,0:T(8,128)} async-done(((f32[32,2048]{1,0:T(8,128)}), f32[32,2048]{1,0:T(8,128)}) %all-reduce.11.cloned.1.call-update) | async-done | bytes 262160 | tf_op jit(solution)/shard_map/psum | solution.py:104
  709.7 1.7 copy.41
  711.4 1.8 copy.42
  713.2 1.7 copy.43
  714.9 1.8 copy.44
  716.7 1.8 copy.45
  718.5 1.7 copy.46
  (104 shorter events, 14.4 us)
Async XLA Ops:
  7.2 93.8 %copy-start = (bf16[32,3584]{1,0:T(8,128)(2,1)S(1)}, bf16[32,3584]{1,0:T(8,128)(2,1)}, u32[]{:S(2)}) copy-start(bf16[32,3584]{1,0:T(8,128)(2,1)} %param.23) | copy-start | bytes 688132
  7.2 35.1 %all-gather.6.cloned.1.call-start = ((), (), s32[]{:S(2)}) async-start(), calls=%async_computation.11 | async-start | bytes 1572864 | tf_op jit(solution)/shard_map/all_gather | solution.py:60
  7.9 33.4 %copy-start.20 = (f32[2048]{0:T(1024)S(1)}, f32[2048]{0:T(1024)}, u32[]{:S(2)}) copy-start(f32[2048]{0:T(1024)} %param.27) | copy-start | bytes 24580
  7.9 33.4 %copy-start.3 = (bf16[128,2048]{1,0:T(8,128)(2,1)S(1)}, bf16[128,2048]{1,0:T(8,128)(2,1)}, u32[]{:S(2)}) copy-start(bf16[128,2048]{1,0:T(8,128)(2,1)} %param.15) | copy-start | bytes 1572868
  7.9 34.4 %copy-start.11 = (bf16[2048,32]{0,1:T(8,128)(2,1)S(1)}, bf16[2048,32]{0,1:T(8,128)(2,1)}, u32[]{:S(2)}) copy-start(bf16[2048,32]{0,1:T(8,128)(2,1)} %param.22) | copy-start | bytes 393220
  8.0 36.8 %copy-start.10 = (bf16[2048,32]{0,1:T(8,128)(2,1)S(1)}, bf16[2048,32]{0,1:T(8,128)(2,1)}, u32[]{:S(2)}) copy-start(bf16[2048,32]{0,1:T(8,128)(2,1)} %param.19) | copy-start | bytes 393220
  8.0 53.0 %copy-start.13 = (bf16[32,2048]{1,0:T(8,128)(2,1)S(1)}, bf16[32,2048]{1,0:T(8,128)(2,1)}, u32[]{:S(2)}) copy-start(bf16[32,2048]{1,0:T(8,128)(2,1)} %param.26) | copy-start | bytes 393220
  8.0 53.0 %all-gather.10.cloned.1.call-start = ((), (), s32[]{:S(2)}) async-start(), calls=%async_computation.17 | async-start | bytes 1572864 | tf_op jit(solution)/shard_map/all_gather | solution.py:107
  42.3 78.0 %reduce-scatter.36.cloned.1.call-start = ((), (), s32[]{:S(2)}) async-start(), calls=%async_computation.26 | async-start | bytes 163840
  44.7 77.0 %reduce-scatter.34.cloned.1.call-start = ((), (), s32[]{:S(2)}) async-start(), calls=%async_computation.25 | async-start | bytes 163840
  47.1 81.6 %reduce-scatter.38.cloned.1.call-start = ((), (), s32[]{:S(2)}) async-start(), calls=%async_computation.27 | async-start | bytes 163840
  63.3 11.5 %copy-start.1 = (bf16[256,2048]{1,0:T(8,128)(2,1)S(1)}, bf16[256,2048]{1,0:T(8,128)(2,1)}, u32[]{:S(2)}) copy-start(bf16[256,2048]{1,0:T(8,128)(2,1)} %all-gather.6.cloned.1.call-done) | copy-start | bytes 3145732
  63.3 109.1 %reduce-scatter.26.cloned.1.call-start = ((), (), s32[]{:S(2)}) async-start(), calls=%async_computation.18 | async-start | bytes 4587520 | tf_op jit(solution)/shard_map/reduce_scatter | solution.py:111
  74.7 141.4 %reduce-scatter.18.cloned.1.call-start = ((), (), s32[]{:S(2)}) async-start(), calls=%async_computation.12 | async-start | bytes 4587520 | tf_op jit(solution)/shard_map/reduce_scatter | solution.py:66
  84.0 9.4 %copy-start.9 = (bf16[32,3584]{1,0:T(8,128)(2,1)S(1)}, bf16[32,3584]{1,0:T(8,128)(2,1)}, u32[]{:S(2)}) copy-start(bf16[32,3584]{1,0:T(8,128)(2,1)} %param.20) | copy-start | bytes 688132
  84.0 176.0 %reduce-scatter.20.cloned.1.call-start = ((), (), s32[]{:S(2)}) async-start(), calls=%async_computation.13 | async-start | bytes 4587520 | tf_op jit(solution)/shard_map/reduce_scatter | solution.py:67
  93.3 191.8 %all-gather.8.cloned.1.call-start = ((), (), s32[]{:S(2)}) async-start(), calls=%async_computation.14 | async-start | bytes 2293760 | tf_op jit(solution)/shard_map/all_gather | solution.py:85
  101.0 18.7 %copy-start.16 = (f32[3584]{0:T(1024)S(1)}, f32[3584]{0:T(1024)}, u32[]{:S(2)}) copy-start(f32[3584]{0:T(1024)} %param.21) | copy-start | bytes 43012
  101.0 18.7 %copy-start.17 = (f32[3584]{0:T(1024)S(1)}, f32[3584]{0:T(1024)}, u32[]{:S(2)}) copy-start(f32[3584]{0:T(1024)} %param.24) | copy-start | bytes 43012
  101.0 71.4 %copy-start.8 = (bf16[3584,32]{0,1:T(8,128)(2,1)S(1)}, bf16[3584,32]{0,1:T(8,128)(2,1)}, u32[]{:S(2)}) copy-start(bf16[3584,32]{0,1:T(8,128)(2,1)} %param.25) | copy-start | bytes 688132
  108.6 280.8 %copy-start.7 = (bf16[128,2048]{1,0:T(8,128)(2,1)S(1)}, bf16[128,2048]{1,0:T(8,128)(2,1)}, u32[]{:S(2)}) copy-start(bf16[128,2048]{1,0:T(8,128)(2,1)} %param.14) | copy-start | bytes 1572868
  263.9 44.4 %all-gather.14.cloned.1.call-start = ((), (), s32[]{:S(2)}) async-start(), calls=%async_computation.20 | async-start | bytes 2293760 | tf_op jit(solution)/shard_map/all_gather | solution.py:140
  264.4 67.0 %all-gather.12.cloned.1.call-start = ((), (), s32[]{:S(2)}) async-start(), calls=%async_computation.19 | async-start | bytes 2293760 | tf_op jit(solution)/shard_map/all_gather | solution.py:139
  265.3 78.7 %reduce-scatter.24.cloned.1.call-start = ((), (), s32[]{:S(2)}) async-start(), calls=%async_computation.16 | async-start | bytes 49152 | tf_op jit(solution)/shard_map/reduce_scatter | solution.py:90
  287.9 69.0 %reduce-scatter.32.cloned.1.call-start = ((), (), s32[]{:S(2)}) async-start(), calls=%async_computation.23 | async-start | bytes 49152 | tf_op jit(solution)/shard_map/reduce_scatter | solution.py:148
  311.0 58.5 %reduce-scatter.30.cloned.1.call-start = ((), (), s32[]{:S(2)}) async-start(), calls=%async_computation.22 | async-start | bytes 49152 | tf_op jit(solution)/shard_map/reduce_scatter | solution.py:147
  334.2 87.4 %all-reduce.17.cloned.1.call-start = ((), (), s32[]{:S(2)}) async-start(), calls=%async_computation.30 | async-start | bytes 1048576 | tf_op jit(solution)/shard_map/psum | solution.py:11
  391.3 11.7 %copy-start.6 = (bf16[256,3584]{1,0:T(8,128)(2,1)S(1)}, bf16[256,3584]{1,0:T(8,128)(2,1)}, u32[]{:S(2)}) copy-start(bf16[256,3584]{1,0:T(8,128)(2,1)} %all-gather.12.cloned.1.call-done) | copy-start | bytes 5505028
  391.3 60.1 %reduce-scatter.22.cloned.1.call-start = ((), (), s32[]{:S(2)}) async-start(), calls=%async_computation.15 | async-start | bytes 3145728 | tf_op jit(solution)/shard_map/reduce_scatter | solution.py:89
  402.9 82.5 %reduce-scatter.28.cloned.1.call-start = ((), (), s32[]{:S(2)}) async-start(), calls=%async_computation.21 | async-start | bytes 3145728 | tf_op jit(solution)/shard_map/reduce_scatter | solution.py:146
  410.3 75.2 %copy-start.2 = (bf16[64,3584]{1,0:T(8,128)(2,1)S(1)}, bf16[64,3584]{1,0:T(8,128)(2,1)}, u32[]{:S(2)}) copy-start(bf16[64,3584]{1,0:T(8,128)(2,1)} %multiply_convert_fusion.3) | copy-start | bytes 1376260
  410.3 76.2 %copy-start.5 = (bf16[64,3584]{1,0:T(8,128)(2,1)S(1)}, bf16[64,3584]{1,0:T(8,128)(2,1)}, u32[]{:S(2)}) copy-start(bf16[64,3584]{1,0:T(8,128)(2,1)} %get-tuple-element.30) | copy-start | bytes 1376260
  410.3 76.2 %copy-start.15 = (bf16[64,32]{0,1:T(8,128)(2,1)S(1)}, bf16[64,32]{0,1:T(8,128)(2,1)}, u32[]{:S(2)}) copy-start(bf16[64,32]{0,1:T(8,128)(2,1)} %copy.28) | copy-start | bytes 12292
  410.3 77.1 %copy-start.4 = (bf16[64,3584]{1,0:T(8,128)(2,1)S(1)}, bf16[64,3584]{1,0:T(8,128)(2,1)}, u32[]{:S(2)}) copy-start(bf16[64,3584]{1,0:T(8,128)(2,1)} %get-tuple-element.31) | copy-start | bytes 1376260
  410.3 78.2 %copy-start.18 = (f32[3584]{0:T(1024)S(1)}, f32[3584]{0:T(1024)}, u32[]{:S(2)}) copy-start(f32[3584]{0:T(1024)} %get-tuple-element.11) | copy-start | bytes 43012
  410.4 78.2 %copy-start.19 = (f32[3584]{0:T(1024)S(1)}, f32[3584]{0:T(1024)}, u32[]{:S(2)}) copy-start(f32[3584]{0:T(1024)} %get-tuple-element.12) | copy-start | bytes 43012
  410.4 181.7 %copy-start.14 = (bf16[32,2048]{1,0:T(8,128)(2,1)S(1)}, bf16[32,2048]{1,0:T(8,128)(2,1)}, u32[]{:S(2)}) copy-start(bf16[32,2048]{1,0:T(8,128)(2,1)} %param.26) | copy-start | bytes 393220
  421.6 194.8 %copy-start.12 = (bf16[2048,32]{0,1:T(8,128)(2,1)S(1)}, bf16[2048,32]{0,1:T(8,128)(2,1)}, u32[]{:S(2)}) copy-start(bf16[2048,32]{0,1:T(8,128)(2,1)} %param.22) | copy-start | bytes 393220
  421.6 170.5 %all-reduce.13.cloned.1.call-start = ((), (), s32[]{:S(2)}) async-start(), calls=%async_computation.28 | async-start | bytes 5242880 | tf_op jit(solution)/shard_map/psum | solution.py:92
  485.4 149.5 %all-reduce.15.cloned.1.call-start = ((), (), s32[]{:S(2)}) async-start(), calls=%async_computation.29 | async-start | bytes 2752512 | tf_op jit(solution)/shard_map/psum | solution.py:127
  488.4 221.3 %all-reduce.11.cloned.1.call-start = ((), (), s32[]{:S(2)}) async-start(), calls=%async_computation.24 | async-start | bytes 524288 | tf_op jit(solution)/shard_map/psum | solution.py:104
Sparse Core Ops, SparseCore 0:
  9.5 24.4 all-gather.5
  42.4 18.5 all-gather.9
  64.0 19.6 reduce-scatter.35
  86.5 19.6 reduce-scatter.33
  109.0 19.6 reduce-scatter.37
  131.1 41.2 reduce-scatter.25
  174.9 41.2 reduce-scatter.17
  218.7 41.2 reduce-scatter.19
  264.0 21.0 all-gather.7
  287.1 21.0 all-gather.13
  310.3 21.0 all-gather.11
  334.1 9.9 reduce-scatter.23
  346.8 9.9 reduce-scatter.31
  359.5 9.9 reduce-scatter.29
  391.4 25.8 all-reduce.16
  419.4 31.8 reduce-scatter.21
  453.5 31.8 reduce-scatter.27
  487.9 104.1 all-reduce.12
  595.8 39.1 all-reduce.14
  638.7 71.0 all-reduce.10
